TPU v7x, 32 devices: a whole 2x2x4 slice. The times are simulated.
32 devices in a mesh: probe: 8 (over y, x, core), tile: 4 (over z).
Axes of the slice: x: 2, y: 2, z: 4, core: 2. Of those that a mesh axis runs over, the one named last changes fastest.
Arguments:
- transmission: bfloat16 [2, 2, 2048, 1024], P(None, None, 'tile', 'probe'), may hold values from -4.1875 to 4.1875
- illumination: bfloat16 [2, 512, 512], replicated, may hold values from -3 to 3
- intensities: float32 [16, 512, 512], P('probe'), may hold values from 0 to 1
- scan_positions: int32 [16, 2], P('probe'), may hold values from 0 to 512, as said below
- tile_owner: int32 [16], P('probe'), may hold values from 0 to 3, as said below
Outputs:
- gradient: float32 [2, 2, 2048, 1024], P(None, None, 'tile', 'probe')
- probe_losses: float32 [16], P('probe')
Inputs may be any that keep to these rules, and one draw needn't show every extreme that they name: `tile_owner`: of the 2 scan positions held by one device along probe, no two have the same owner. scan_positions[k, 0] counts rows from row tile_owner[k] * 512 - 128 of the object and scan_positions[k, 1] columns from its first column; the 512 x 512 window of every probe lies inside the object and inside its owner's rows widened by 128 on each side.
All inputs are finite; a program needn't handle non-finite values.
Results may differ from a plain program's by a relative error of at most 0.012.
Values may be sent and summed in bfloat16 or wider, within the bound.
A program may use at most 128 MiB of HBM per device.

v0:
```python
import functools
import math

import jax
import jax.numpy as jnp
import numpy as np
from jax import lax
from jax.experimental import pallas as pl
from jax.experimental.pallas import tpu as pltpu
from jax.sharding import PartitionSpec as P

BORDER = 128
FRESNEL = 0.25
F32 = jnp.float32
BF16 = jnp.bfloat16


def tables_of(n):
    k = np.arange(n)
    angle = -2.0 * np.pi * ((k[:, None] * k[None, :]) % n) / n
    wave = np.exp(1j * angle) / math.sqrt(n)
    freq = np.where(k < n // 2, k, k - n).astype(np.float64)
    h = np.exp(-1j * np.pi * FRESNEL * freq * freq / n)
    q = np.fft.ifft(h)
    prop = q[(k[:, None] - k[None, :]) % n]
    return [jnp.asarray(np.asarray(t, np.float32).astype(jnp.bfloat16))
            for t in (wave.real, wave.imag, prop.real, prop.imag)]


def compute_kernel(pos, band, illum, meas, wr, wi, qr, qi, out, loss,
                   wide, x0, x1, obj, er, ei, ir, ii, msc, msem):
    n = illum.shape[-1]
    slices = band.shape[0]
    assert slices == 2
    step = n // 2
    row0, col0, usable, chosen = pos[0], pos[1], pos[2], pos[3]
    extra = band.shape[2] - n

    @pl.when(usable == 0)
    def _():
        loss[...] = jnp.zeros_like(loss)
        for s in range(slices):
            for c in range(2):
                out[s, c] = jnp.zeros(out.shape[2:], out.dtype)

    def chunks(fn):
        def body(i, carry):
            fn(pl.multiple_of(i * step, step))
            return carry
        lax.fori_loop(0, n // step, body, 0)

    def transform(tr, ti, sign, emit):
        def right(r):
            a, b = er[pl.ds(r, step), :], ei[pl.ds(r, step), :]
            dot = functools.partial(jnp.dot, preferred_element_type=F32)
            rr, mm = dot(a, tr[...]), dot(b, ti[...])
            ir[pl.ds(r, step), :] = (rr - mm if sign > 0 else rr + mm).astype(BF16)
            rm, mr = dot(a, ti[...]), dot(b, tr[...])
            ii[pl.ds(r, step), :] = (mr + rm if sign > 0 else mr - rm).astype(BF16)

        chunks(right)

        def left(r):
            a, b = tr[pl.ds(r, step), :], ti[pl.ds(r, step), :]
            dot = functools.partial(jnp.dot, preferred_element_type=F32)
            rr, mm = dot(a, ir[...]), dot(b, ii[...])
            rm, mr = dot(a, ii[...]), dot(b, ir[...])
            emit(r, rr - mm if sign > 0 else rr + mm, rm + mr if sign > 0 else rm - mr)

        chunks(left)

    @pl.when(usable != 0)
    def _():
        fetch = pltpu.make_async_copy(meas.at[chosen], msc, msem)
        fetch.start()
        for c in range(2):
            for r in range(0, n, 64):
                turned = pltpu.roll(illum[c, r:r + 64, :].astype(F32), col0 & (n - 1), 1)
                wide[r:r + 64, :] = turned
                wide[n + r:n + r + 64, :] = turned
            base = (n - row0) // 8 * 8
            turn = (72 - (n - row0 - base)) % 72
            for r in range(0, n, 64):
                lines = wide[pl.ds(pl.multiple_of(base + r, 8), 72), :]
                x0[c, r:r + 64, :] = pltpu.roll(lines, turn, 0)[:64]

        col = lax.broadcasted_iota(jnp.int32, (64, n), 1)
        line = lax.broadcasted_iota(jnp.int32, (64, n), 0)
        for s in range(slices):
            for r in range(0, n, 64):
                part = []
                for c in range(2):
                    low = jnp.where(col < col0, band[s, c, r:r + 64, n:].astype(F32),
                                    band[s, c, r:r + 64, :n].astype(F32))
                    if r < extra:
                        high = jnp.where(col < col0, band[s, c, n + r:n + r + 64, n:].astype(F32),
                                         band[s, c, n + r:n + r + 64, :n].astype(F32))
                        low = jnp.where(line + r < row0, high, low)
                    part.append(low)
                a, b = part
                if s == 0:
                    u, v = x0[0, r:r + 64, :], x0[1, r:r + 64, :]
                    er[r:r + 64, :] = (u * a - v * b).astype(BF16)
                    ei[r:r + 64, :] = (u * b + v * a).astype(BF16)
                else:
                    obj[0, r:r + 64, :] = a.astype(BF16)
                    obj[1, r:r + 64, :] = b.astype(BF16)

        def emit_first(r, re, im):
            rows = pl.ds(r, step)
            x1[0, rows, :] = re
            x1[1, rows, :] = im
            a, b = obj[0, rows, :].astype(F32), obj[1, rows, :].astype(F32)
            er[rows, :] = (re * a - im * b).astype(BF16)
            ei[rows, :] = (re * b + im * a).astype(BF16)

        transform(qr, qi, 1, emit_first)
        fetch.wait()
        loss[...] = jnp.zeros_like(loss)

        def emit_far(r, re, im):
            rows = pl.ds(r, step)
            misfit = re * re + im * im - msc[rows, :]
            sq = jnp.sum((misfit * misfit).reshape(step // 8, 8, n), axis=0)
            loss[...] += functools.reduce(jnp.add, [sq[:, j:j + 128] for j in range(0, n, 128)])
            er[rows, :] = (misfit * re).astype(BF16)
            ei[rows, :] = (misfit * im).astype(BF16)

        transform(wr, wi, 1, emit_far)

        def place(s, r, parts):
            col = lax.broadcasted_iota(jnp.int32, (step, n), 1)
            line = lax.broadcasted_iota(jnp.int32, (step, n), 0) + r
            for c, g in enumerate(parts):
                keep = jnp.where(line >= row0, g, 0.0)
                out[s, c, pl.ds(r, step), :n] = jnp.where(col >= col0, keep, 0.0).astype(BF16)
                out[s, c, pl.ds(r, step), n:] = jnp.where(col < col0, keep, 0.0).astype(BF16)

                @pl.when(r < extra)
                def _():
                    for j in range(0, extra, step):
                        over = jnp.where(line < row0, g, 0.0)
                        out[s, c, n + j:n + j + step, :n] = jnp.where(col >= col0, over, 0.0).astype(BF16)
                        out[s, c, n + j:n + j + step, n:] = jnp.where(col < col0, over, 0.0).astype(BF16)

        def emit_back(r, re, im):
            rows = pl.ds(r, step)
            u, v = x1[0, rows, :], x1[1, rows, :]
            place(1, r, (u * re + v * im, u * im - v * re))
            a, b = obj[0, rows, :].astype(F32), obj[1, rows, :].astype(F32)
            er[rows, :] = (a * re + b * im).astype(BF16)
            ei[rows, :] = (a * im - b * re).astype(BF16)

        transform(wr, wi, -1, emit_back)

        def emit_last(r, re, im):
            rows = pl.ds(r, step)
            u, v = x0[0, rows, :], x0[1, rows, :]
            place(0, r, (u * re + v * im, u * im - v * re))

        transform(qr, qi, -1, emit_last)


def compute(pos, band, illumination, intensities):
    n = illumination.shape[-1]
    vmem = pl.BlockSpec(memory_space=pltpu.VMEM)
    return pl.pallas_call(
        compute_kernel,
        out_shape=(jax.ShapeDtypeStruct(band.shape, BF16), jax.ShapeDtypeStruct((8, 128), F32)),
        in_specs=[pl.BlockSpec(memory_space=pltpu.SMEM), vmem, vmem,
                  pl.BlockSpec(memory_space=pl.ANY)] + [vmem] * 4,
        out_specs=(vmem, vmem),
        scratch_shapes=[
            pltpu.VMEM((2 * n + 8, n), F32), pltpu.VMEM((2, n, n), F32), pltpu.VMEM((2, n, n), F32),
            pltpu.VMEM((2, n, n), BF16)] + [pltpu.VMEM((n, n), BF16)] * 4 + [
            pltpu.VMEM((n, n), F32), pltpu.SemaphoreType.DMA],
        compiler_params=pltpu.CompilerParams(vmem_limit_bytes=56 << 20),
        name="probe_pass",
    )(pos, band, illumination, intensities, *tables_of(n))


def extended(value, axis, dim, width):
    size, length = lax.axis_size(axis), value.shape[dim]
    up = [(i, i + 1) for i in range(size - 1)]
    down = [(j, i) for i, j in up]
    before = lax.ppermute(lax.slice_in_dim(value, length - width, length, axis=dim), axis, up)
    after = lax.ppermute(lax.slice_in_dim(value, 0, width, axis=dim), axis, down)
    return jnp.concatenate([before, value, after], axis=dim)


def body(transmission, illumination, intensities, scan_positions, tile_owner):
    tile_index = lax.axis_index("tile")
    tile_rows = transmission.shape[2]
    n = illumination.shape[-1]
    owned = tile_owner == tile_index
    chosen = jnp.argmax(owned).astype(jnp.int32)
    usable = jnp.any(owned)
    place = jnp.sum(jnp.where(owned[:, None], scan_positions, 0), axis=0)
    pos = jnp.stack([place[0], place[1], usable.astype(jnp.int32), chosen])
    band = lax.all_gather(extended(transmission, "tile", 2, BORDER), "probe", axis=3, tiled=True)
    summed, loss = compute(pos, band, illumination, intensities)
    wide = lax.psum_scatter(summed, "probe", scatter_dimension=3, tiled=True).astype(F32)
    size = lax.axis_size("tile")
    up = [(i, i + 1) for i in range(size - 1)]
    down = [(j, i) for i, j in up]
    from_above = lax.ppermute(wide[:, :, :BORDER].astype(BF16), "tile", down).astype(F32)
    from_below = lax.ppermute(wide[:, :, tile_rows + BORDER:].astype(BF16), "tile", up).astype(F32)
    interior = wide[:, :, BORDER:BORDER + tile_rows]
    interior = interior.at[:, :, tile_rows - BORDER:].add(from_above)
    interior = interior.at[:, :, :BORDER].add(from_below)
    local = jnp.where(owned, jnp.sum(loss) / (n * n), 0.0)
    return interior, lax.psum(local, "tile")


def solution(mesh):
    in_specs = (P(None, None, "tile", "probe"), P(), P("probe", None, None), P("probe", None), P("probe"))
    out_specs = (P(None, None, "tile", "probe"), P("probe"))
    return jax.shard_map(body, mesh=mesh, in_specs=in_specs, out_specs=out_specs, check_vma=False)
```

profile of v0, /device:TPU:0, one launch (start us, length us, event | category | flops | bytes accessed | tf_op | source)
XLA Modules:
  0.0 214.0 jit_solution(10149448807366358994)
XLA Ops:
  7.2 0.0 copy-start.3
  7.2 0.0 copy-start.2
  7.2 0.0 all-gather.2.cloned.1.call-start
  7.2 1.0 fusion.4
  8.2 5.0 %collective-permute-start = (bf16[2,2,128,128]{3,2,1,0:T(8,128)(2,1)S(1)}, bf16[2,2,128,128]{3,2,1,0:T(8,128)(2,1)S(1)}, u32[]{:S(2)}, u32[]{:S(2)}) collective-permute-start(bf16[2,2,128,128]{3,2,1,0:T(8,128)(2,1)S(1)} %get-tuple-element.36), channel_id=1, source_target_pairs={{0,1},{1,2},{2,3},{4,5},{5,6},{6,7},{8,9},{9,10},{10,11},{12,13},{... | collective-permute-start | bytes 393224 | tf_op jit(solution)/shard_map/ppermute | solution.py:186
  13.2 1.3 collective-permute-start.1
  14.5 1.4 collective-permute-done
  15.9 4.1 %collective-permute-done.1 = bf16[2,2,128,128]{3,2,1,0:T(8,128)(2,1)S(1)} collective-permute-done((bf16[2,2,128,128]{3,2,1,0:T(8,128)(2,1)S(1)}, bf16[2,2,128,128]{3,2,1,0:T(8,128)(2,1)S(1)}, u32[]{:S(2)}, u32[]{:S(2)}) %collective-permute-start.1) | collective-permute-done | bytes 131104 | tf_op jit(solution)/shard_map/ppermute | solution.py:187
  20.1 2.0 pad_maximum_fusion
  22.0 0.0 all-gather.2.cloned.1.call-update
  22.1 0.0 reduce-scatter.4.cloned.1.call-start
  22.1 0.0 copy-done.3
  22.1 0.6 fusion.2
  23.4 0.0 copy-done.2
  23.4 0.1 select_reduce_fusion
  23.5 0.7 iota_reduce_fusion
  24.2 1.2 pad_add_fusion.pos
  25.3 43.7 %all-gather.2.cloned.1.call-done.band = bf16[2,2,768,1024]{3,2,1,0:T(8,128)(2,1)} async-done(((bf16[2,2,768,128]{3,2,1,0:T(8,128)(2,1)}), bf16[2,2,768,1024]{3,2,1,0:T(8,128)(2,1)}) %all-gather.2.cloned.1.call-update) | async-done | bytes 6291472 | tf_op jit(solution)/shard_map/all_gather | solution.py:200
  69.0 22.1 %probe_pass.1 = (bf16[2,2,768,1024]{3,2,1,0:T(8,128)(2,1)}, f32[8,128]{1,0:T(8,128)}) custom-call(s32[4]{0:T(128)} %pad_add_fusion.pos, bf16[2,2,768,1024]{3,2,1,0:T(8,128)(2,1)} %all-gather.2.cloned.1.call-done.band, bf16[2,512,512]{2,1,0:T(8,128)(2,1)} %illum.1, f32[2,512,512]{2,1,0:T(8,128)} %meas.1, bf16[512,512]{1,0:T(8,128)(2,1)} %constant.79.clone.wr, ...), custom_call_target="tpu_custom_call" | custom-call | tf_op jit(solution)/shard_map/probe_pass/pallas_call | solution.py:167
  91.1 16.4 %copy.11 = bf16[2,2,768,1024]{2,1,0,3:T(2,128)(2,1)} copy(bf16[2,2,768,1024]{3,2,1,0:T(8,128)(2,1)} %get-tuple-element.30) | data formatting | bytes 12582912
  107.6 14.4 %reshape.76 = bf16[1024,3072]{1,0:T(8,128)(2,1)} reshape(bf16[1024,2,2,768]{3,2,1,0:T(2,128)(2,1)} %bitcast.4) | data formatting | bytes 12582912
  122.0 0.0 copy-start.1
  122.0 0.0 reduce-scatter.4.cloned.1.call-update
  122.0 0.7 copy-done.1
  122.7 0.6 reduce_sum.19
  123.9 60.0 %reduce-scatter.4.cloned.1.call-done = bf16[128,3072]{1,0:T(8,128)(2,1)} async-done(((bf16[1024,3072]{1,0:T(8,128)(2,1)}), bf16[128,3072]{1,0:T(8,128)(2,1)}) %reduce-scatter.4.cloned.1.call-update) | async-done | bytes 786448
  183.9 2.6 %reshape.77 = bf16[128,2,2,768]{3,2,1,0:T(2,128)(2,1)S(1)} reshape(bf16[128,3072]{1,0:T(8,128)(2,1)} %reduce-scatter.4.cloned.1.call-done) | data formatting | bytes 1572864
  186.5 0.9 copy.12
  187.5 1.3 collective-permute-start.2
  188.8 13.4 %psum.7 = f32[2]{0:T(128)} all-reduce(f32[2]{0:T(128)S(1)} %broadcast_select_fusion), channel_id=1, replica_groups=mesh['probe'=8,'tile'=4] {'tile'}, use_global_device_ids=true, to_apply=%region_5.6 | all-reduce | flops 2 | bytes 16 | tf_op jit(solution)/shard_map/psum | solution.py:212
  202.1 0.1 slice.86
  202.2 0.1 convert_element_type.12
  202.3 1.3 collective-permute-start.3
  203.6 0.0 collective-permute-done.2
  203.7 2.5 %collective-permute-done.3 = bf16[2,2,128,128]{3,2,1,0:T(8,128)(2,1)S(1)} collective-permute-done((bf16[2,2,128,128]{3,2,1,0:T(8,128)(2,1)S(1)}, bf16[2,2,128,128]{3,2,1,0:T(8,128)(2,1)S(1)}, u32[]{:S(2)}, u32[]{:S(2)}) %collective-permute-start.3) | collective-permute-done | bytes 131104 | tf_op jit(solution)/shard_map/ppermute | solution.py:207
  206.1 0.1 fusion
  206.2 0.0 copy-start
  206.2 1.0 copy-done
  (3 shorter events, 0.1 us)
Async XLA Ops:
  7.2 15.0 %copy-start.3 = (s32[2]{0:T(128)S(1)}, s32[2]{0:T(128)}, u32[]{:S(2)}) copy-start(s32[2]{0:T(128)} %param.17) | copy-start | bytes 28
  7.2 16.2 %copy-start.2 = (s32[2,2]{1,0:T(2,128)S(1)}, s32[2,2]{1,0:T(2,128)}, u32[]{:S(2)}) copy-start(s32[2,2]{1,0:T(2,128)} %param.16) | copy-start | bytes 52
  7.2 61.9 %all-gather.2.cloned.1.call-start = ((), (), s32[]{:S(2)}) async-start(), calls=%async_computation.1 | async-start | bytes 7077888 | tf_op jit(solution)/shard_map/all_gather | solution.py:200
  8.2 7.7 %collective-permute-start = (bf16[2,2,128,128]{3,2,1,0:T(8,128)(2,1)S(1)}, bf16[2,2,128,128]{3,2,1,0:T(8,128)(2,1)S(1)}, u32[]{:S(2)}, u32[]{:S(2)}) collective-permute-start(bf16[2,2,128,128]{3,2,1,0:T(8,128)(2,1)S(1)} %get-tuple-element.36), channel_id=1, source_target_pairs={{0,1},{1,2},{2,3},{4,5},{5,6},{6,7},{8,9},{9,10},{10,11},{12,13},{... | collective-permute-start | bytes 393224 | tf_op jit(solution)/shard_map/ppermute | solution.py:186
  13.2 6.9 %collective-permute-start.1 = (bf16[2,2,128,128]{3,2,1,0:T(8,128)(2,1)S(1)}, bf16[2,2,128,128]{3,2,1,0:T(8,128)(2,1)S(1)}, u32[]{:S(2)}, u32[]{:S(2)}) collective-permute-start(bf16[2,2,128,128]{3,2,1,0:T(8,128)(2,1)S(1)} %get-tuple-element.37), channel_id=1, source_target_pairs={{1,0},{2,1},{3,2},{5,4},{6,5},{7,6},{9,8},{10,9},{11,10},{13,12},{... | collective-permute-start | bytes 393224 | tf_op jit(solution)/shard_map/ppermute | solution.py:187
  22.1 161.9 %reduce-scatter.4.cloned.1.call-start = ((), (), s32[]{:S(2)}) async-start(), calls=%async_computation.2 | async-start | bytes 7077888
  122.0 0.7 copy-start.1
  187.5 16.2 %collective-permute-start.2 = (bf16[2,2,128,128]{3,2,1,0:T(8,128)(2,1)S(1)}, bf16[2,2,128,128]{3,2,1,0:T(8,128)(2,1)S(1)}, u32[]{:S(2)}, u32[]{:S(2)}) collective-permute-start(bf16[2,2,128,128]{3,2,1,0:T(8,128)(2,1)S(1)} %get-tuple-element.35), channel_id=1, source_target_pairs={{1,0},{2,1},{3,2},{5,4},{6,5},{7,6},{9,8},{10,9},{11,10},{13,12},{... | collective-permute-start | bytes 393224 | tf_op jit(solution)/shard_map/ppermute | solution.py:206
  202.3 3.8 %collective-permute-start.3 = (bf16[2,2,128,128]{3,2,1,0:T(8,128)(2,1)S(1)}, bf16[2,2,128,128]{3,2,1,0:T(8,128)(2,1)S(1)}, u32[]{:S(2)}, u32[]{:S(2)}) collective-permute-start(bf16[2,2,128,128]{3,2,1,0:T(8,128)(2,1)S(1)} %get-tuple-element.34), channel_id=1, source_target_pairs={{0,1},{1,2},{2,3},{4,5},{5,6},{6,7},{8,9},{9,10},{10,11},{12,13},{... | collective-permute-start | bytes 393224 | tf_op jit(solution)/shard_map/ppermute | solution.py:207
  206.2 1.0 copy-start
Sparse Core Ops, SparseCore 0:
  22.2 46.8 all-gather.1
  122.1 61.7 reduce-scatter.3
where the time goes:
time: 215 us; the launch traced here: 214 us
  waiting for transfers between devices  112 us (52%)
  local copies, waits for them, and re-layouts  37.1 us (17%)
  Pallas kernels  22.1 us (10%)
  between operations  15.5 us (7%)
  blocking collectives  13.4 us (6%)
  starting transfers between devices  8.92 us (4%)
  other arithmetic  5.3 us (2%)
    unnamed x3, waiting for transfers between devices  60 us
    all_gather x1, waiting for transfers between devices, body(): lax.all_gather(extended(transmission, 'tile', 2, BORDER), 'probe', axis=3...  43.7 us
    unnamed x12, local copies, waits for them, and re-layouts  36 us
    pallas_call x1, Pallas kernels, compute(): pl.pallas_call(compute_kernel, out_shape=(jax.ShapeDtypeStruct(band.shape...  22.1 us
    psum x1, blocking collectives, body(): return (interior, lax.psum(local, 'tile'))  13.4 us
    ppermute x1, starting transfers between devices, extended(): lax.ppermute(lax.slice_in_dim(value, length - width, length, axis=dim), a...  4.96 us
  transfers between devices with their start and end apart: 6, of which 5 were waited for; matrix products, arithmetic and copies ran while one was open for 2% of the time, Pallas kernels for 0%

commit v1 on v0

v1 whole, which is shorter than its diff:
```python
import functools
import math

import jax
import jax.numpy as jnp
import numpy as np
from jax import lax
from jax.experimental import pallas as pl
from jax.experimental.pallas import tpu as pltpu
from jax.sharding import PartitionSpec as P

BORDER = 128
FRESNEL = 0.25
F32 = jnp.float32
BF16 = jnp.bfloat16


def tables_of(n):
    k = np.arange(n)
    angle = -2.0 * np.pi * ((k[:, None] * k[None, :]) % n) / n
    wave = np.exp(1j * angle) / math.sqrt(n)
    freq = np.where(k < n // 2, k, k - n).astype(np.float64)
    h = np.exp(-1j * np.pi * FRESNEL * freq * freq / n)
    q = np.fft.ifft(h)
    prop = q[(k[:, None] - k[None, :]) % n]
    return [jnp.asarray(np.asarray(t, np.float32).astype(jnp.bfloat16))
            for t in (wave.real, wave.imag, prop.real, prop.imag)]


def compute_kernel(pos, fold, illum, meas, wr, wi, qr, qi, out, loss,
                   wide, x0, x1, obj, er, ei, ir, ii, msc, msem):
    n = illum.shape[-1]
    blocks, slices, width = fold.shape[0], fold.shape[1], fold.shape[-1]
    assert slices == 2
    step = n // 2
    row0, col0, usable, chosen = pos[0], pos[1], pos[2], pos[3]

    @pl.when(usable == 0)
    def _():
        loss[...] = jnp.zeros_like(loss)
        out[...] = jnp.zeros_like(out)

    def chunks(fn):
        def body(i, carry):
            fn(pl.multiple_of(i * step, step))
            return carry
        lax.fori_loop(0, n // step, body, 0)

    def transform(tr, ti, sign, emit):
        dot = functools.partial(jnp.dot, preferred_element_type=F32)

        def right(r):
            a, b = er[pl.ds(r, step), :], ei[pl.ds(r, step), :]
            rr, mm = dot(a, tr[...]), dot(b, ti[...])
            ir[pl.ds(r, step), :] = (rr - mm if sign > 0 else rr + mm).astype(BF16)
            rm, mr = dot(a, ti[...]), dot(b, tr[...])
            ii[pl.ds(r, step), :] = (mr + rm if sign > 0 else mr - rm).astype(BF16)

        chunks(right)

        def left(r):
            a, b = tr[pl.ds(r, step), :], ti[pl.ds(r, step), :]
            rr, mm = dot(a, ir[...]), dot(b, ii[...])
            rm, mr = dot(a, ii[...]), dot(b, ir[...])
            emit(r, rr - mm if sign > 0 else rr + mm, rm + mr if sign > 0 else rm - mr)

        chunks(left)

    @pl.when(usable != 0)
    def _():
        fetch = pltpu.make_async_copy(meas.at[chosen], msc, msem)
        fetch.start()
        wide[2 * n:, :] = jnp.zeros((8, n), F32)
        base = (n - row0) // 8 * 8
        turn = (72 - (n - row0 - base)) % 72
        for c in range(2):
            for r in range(0, n, 64):
                turned = pltpu.roll(illum[c, r:r + 64, :].astype(F32), col0 & (n - 1), 1)
                wide[r:r + 64, :] = turned
                wide[n + r:n + r + 64, :] = turned
            for r in range(0, n, 64):
                lines = wide[pl.ds(pl.multiple_of(base + r, 8), 72), :]
                x0[c, r:r + 64, :] = pltpu.roll(lines, turn, 0)[:64]

        for j in range(blocks):
            cols = slice(j * width, (j + 1) * width)
            for r in range(0, n, 128):
                rows = slice(r, r + 128)
                a, b = fold[j, 0, 0, rows].astype(F32), fold[j, 0, 1, rows].astype(F32)
                u, v = x0[0, rows, cols], x0[1, rows, cols]
                er[rows, cols] = (u * a - v * b).astype(BF16)
                ei[rows, cols] = (u * b + v * a).astype(BF16)
            obj[:, :, cols] = fold[j, 1]

        def emit_first(r, re, im):
            rows = pl.ds(r, step)
            x1[0, rows, :] = re
            x1[1, rows, :] = im
            a, b = obj[0, rows, :].astype(F32), obj[1, rows, :].astype(F32)
            er[rows, :] = (re * a - im * b).astype(BF16)
            ei[rows, :] = (re * b + im * a).astype(BF16)

        transform(qr, qi, 1, emit_first)
        fetch.wait()
        loss[...] = jnp.zeros_like(loss)

        def emit_far(r, re, im):
            rows = pl.ds(r, step)
            misfit = re * re + im * im - msc[rows, :]
            sq = jnp.sum((misfit * misfit).reshape(step // 8, 8, n), axis=0)
            loss[...] += functools.reduce(jnp.add, [sq[:, j:j + 128] for j in range(0, n, 128)])
            er[rows, :] = (misfit * re).astype(BF16)
            ei[rows, :] = (misfit * im).astype(BF16)

        transform(wr, wi, 1, emit_far)
        slot = lax.broadcasted_iota(jnp.int32, loss.shape, 0)
        loss[...] = jnp.where(slot == chosen, jnp.sum(loss[...]) / (n * n), 0.0)

        def place(s, r, parts):
            for c, g in enumerate(parts):
                for j in range(blocks):
                    out[j, s, c, pl.ds(r, step), :] = g[:, j * width:(j + 1) * width].astype(BF16)

        def emit_back(r, re, im):
            rows = pl.ds(r, step)
            u, v = x1[0, rows, :], x1[1, rows, :]
            place(1, r, (u * re + v * im, u * im - v * re))
            a, b = obj[0, rows, :].astype(F32), obj[1, rows, :].astype(F32)
            er[rows, :] = (a * re + b * im).astype(BF16)
            ei[rows, :] = (a * im - b * re).astype(BF16)

        transform(wr, wi, -1, emit_back)

        def emit_last(r, re, im):
            rows = pl.ds(r, step)
            u, v = x0[0, rows, :], x0[1, rows, :]
            place(0, r, (u * re + v * im, u * im - v * re))

        transform(qr, qi, -1, emit_last)


def compute(pos, fold, illumination, intensities):
    n = illumination.shape[-1]
    vmem = pl.BlockSpec(memory_space=pltpu.VMEM)
    return pl.pallas_call(
        compute_kernel,
        out_shape=(jax.ShapeDtypeStruct(fold.shape, BF16), jax.ShapeDtypeStruct((8, 128), F32)),
        in_specs=[pl.BlockSpec(memory_space=pltpu.SMEM), vmem, vmem,
                  pl.BlockSpec(memory_space=pl.ANY)] + [vmem] * 4,
        out_specs=(vmem, vmem),
        scratch_shapes=[
            pltpu.VMEM((2 * n + 8, n), F32), pltpu.VMEM((2, n, n), F32), pltpu.VMEM((2, n, n), F32),
            pltpu.VMEM((2, n, n), BF16)] + [pltpu.VMEM((n, n), BF16)] * 4 + [
            pltpu.VMEM((n, n), F32), pltpu.SemaphoreType.DMA],
        compiler_params=pltpu.CompilerParams(vmem_limit_bytes=40 << 20),
        name="probe_pass",
    )(pos, fold, illumination, intensities, *tables_of(n))


MESH = pl.DeviceIdType.MESH


class Places:
    def __init__(self, group):
        self.group, self.tiles = group, lax.axis_size("tile")
        self.me, self.tile = lax.axis_index("probe"), lax.axis_index("tile")
        self.half, self.block = self.me // group, lax.rem(self.me, group)
        self.partner = (lax.rem(self.me + group, 2 * group), self.tile)

    def peer(self, off):
        return (self.half * self.group + lax.rem(self.block + off, self.group), self.tile)

    def tile_peer(self, off):
        return (self.me, lax.rem(self.tile + off, self.tiles))

    def meet(self):
        barrier = pltpu.get_barrier_semaphore()
        others = ([self.partner] + [self.peer(o) for o in range(1, self.group)]
                  + [self.tile_peer(o) for o in range(1, self.tiles)])
        for other in others:
            pl.semaphore_signal(barrier, inc=1, device_id=other, device_id_type=MESH)
        pl.semaphore_wait(barrier, len(others))


def remote(src, dst, send, recv, device):
    return pltpu.make_async_remote_copy(src_ref=src, dst_ref=dst, send_sem=send, recv_sem=recv,
                                        device_id=device, device_id_type=MESH)


def collect_kernel(group, tr, pos, fold, posall, ext, sbuf, psend, precv, zsend, zrecv,
                   ysend, yrecv, xsend, xrecv):
    slices, _, rows, width = tr.shape
    n = fold.shape[-2]
    extra = 2 * BORDER
    at = Places(group)
    at.meet()
    pcopies = [remote(pos, posall.at[o], psend.at[o], precv.at[o], at.peer(o)) for o in range(1, group)]
    for copy in pcopies:
        copy.start()
    top, low = slice(0, BORDER), slice(BORDER + rows, BORDER + rows + BORDER)
    mid = slice(BORDER, BORDER + rows)
    down = remote(tr.at[:, :, rows - BORDER:], ext.at[:, 0, :, top], zsend.at[0], zrecv.at[0], at.tile_peer(1))
    up = remote(tr.at[:, :, :BORDER], ext.at[:, 0, :, low], zsend.at[1], zrecv.at[1], at.tile_peer(at.tiles - 1))
    first, last = at.tile == 0, at.tile == at.tiles - 1

    @pl.when(jnp.logical_not(last))
    def _():
        down.start()

    @pl.when(jnp.logical_not(first))
    def _():
        up.start()

    ymid = [remote(tr.at[s], ext.at[s, 1, :, mid], ysend.at[s, 0], yrecv.at[s, 0], at.partner)
            for s in range(slices)]
    ymid[0].start()
    posall[0] = pos[...]
    for s in range(slices):
        ext[s, 0, :, mid, :] = tr[s]

    @pl.when(first)
    def _():
        ext[:, 0, :, top, :] = jnp.zeros((slices, 2, BORDER, width), BF16)

    @pl.when(last)
    def _():
        ext[:, 0, :, low, :] = jnp.zeros((slices, 2, BORDER, width), BF16)

    @pl.when(jnp.logical_not(first))
    def _():
        down.wait_recv()

    @pl.when(jnp.logical_not(last))
    def _():
        up.wait_recv()

    yends = []
    for s in range(slices):
        if s:
            ymid[s].start()
        pair = [remote(ext.at[s, 0, :, part], ext.at[s, 1, :, part], ysend.at[s, 1 + i], yrecv.at[s, 1 + i], at.partner)
                for i, part in enumerate((top, low))]
        for copy in pair:
            copy.start()
        yends.append(pair)
    for copy in pcopies:
        copy.wait_recv()
    lane = lax.broadcasted_iota(jnp.int32, (extra, width), 1) + at.block * width
    line = lax.broadcasted_iota(jnp.int32, (extra, width), 0)
    xcopies = []
    for s in range(slices):
        for copy in (ymid[s], *yends[s]):
            copy.wait_recv()
        for o in list(range(1, group)) + [0]:
            who = posall[(group - o) % group]
            row0, col0 = who[0:1, :width], who[1:2, :width]
            mine = jnp.where(lane < col0, 1, 0) == at.half
            for c in range(2):
                for r in range(0, n, extra):
                    v = jnp.where(mine, ext[s, 0, c, r:r + extra].astype(F32), ext[s, 1, c, r:r + extra].astype(F32))
                    if r + n < rows + extra:
                        w = jnp.where(mine, ext[s, 0, c, n + r:n + r + extra].astype(F32),
                                      ext[s, 1, c, n + r:n + r + extra].astype(F32))
                        v = jnp.where(line + r < row0, w, v)
                    if o:
                        sbuf[s, o, c, r:r + extra, :] = v.astype(BF16)
                    else:
                        fold[at.block, s, c, r:r + extra, :] = v.astype(BF16)
            if o:
                copy = remote(sbuf.at[s, o], fold.at[at.block, s], xsend.at[s, o], xrecv.at[s, o], at.peer(o))
                copy.start()
                xcopies.append(copy)
    for copy in pcopies + xcopies:
        copy.wait_send()
    for copy in xcopies:
        copy.wait_recv()
    for s in range(slices):
        for copy in (ymid[s], *yends[s]):
            copy.wait_send()

    @pl.when(jnp.logical_not(last))
    def _():
        down.wait_send()

    @pl.when(jnp.logical_not(first))
    def _():
        up.wait_send()


def collect(transmission, postile, n):
    slices, _, rows, width = transmission.shape
    group = n // width
    vmem = pl.BlockSpec(memory_space=pltpu.VMEM)
    dma = pltpu.SemaphoreType.DMA
    return pl.pallas_call(
        functools.partial(collect_kernel, group),
        out_shape=(jax.ShapeDtypeStruct((group, slices, 2, n, width), BF16),
                   jax.ShapeDtypeStruct((group, 8, 128), jnp.int32)),
        in_specs=[vmem, vmem], out_specs=(vmem, vmem),
        scratch_shapes=[
            pltpu.VMEM((slices, 2, 2, rows + 2 * BORDER, width), BF16),
            pltpu.VMEM((slices, group, 2, n, width), BF16),
            dma((group,)), dma((group,)), dma((2,)), dma((2,)), dma((slices, 3)), dma((slices, 3)),
            dma((slices, group)), dma((slices, group))],
        compiler_params=pltpu.CompilerParams(collective_id=0, has_side_effects=True, vmem_limit_bytes=24 << 20),
        name="collect",
    )(transmission, postile)


def spread_kernel(group, grad, posall, loss, out, losses, rbuf, keep, sbuf, ybuf, zout, zin, lbuf,
                  lsend, lrecv, zsend, zrecv, ysend, yrecv, xsend, xrecv):
    slices, _, rows, width = out.shape
    n = grad.shape[-2]
    at = Places(group)
    at.meet()
    order = list(range(slices - 1, -1, -1))
    xcopies = {}
    for s in order:
        for o in range(1, group):
            peer = lax.rem(at.block + o, group)
            xcopies[s, o] = remote(grad.at[peer, s], rbuf.at[s, o], xsend.at[s, o], xrecv.at[s, o], at.peer(o))
            xcopies[s, o].start()
    lcopies = [remote(loss, lbuf.at[o], lsend.at[o], lrecv.at[o], at.tile_peer(o)) for o in range(1, at.tiles)]
    for copy in lcopies:
        copy.start()
    lane = lax.broadcasted_iota(jnp.int32, (BORDER, width), 1) + at.block * width
    line = lax.broadcasted_iota(jnp.int32, (BORDER, width), 0)
    ycopies = {}
    for s in order:
        for o in range(1, group):
            xcopies[s, o].wait_recv()
        for away in (True, False):
            cols = lane + (1 - at.half if away else at.half) * n
            for c in range(2):
                for r in range(0, rows + 2 * BORDER, BORDER):
                    total = None
                    for o in range(group):
                        who = posall[o]
                        row0, col0 = who[0:1, :width], who[1:2, :width]
                        inside = (cols >= col0) & (cols < col0 + n) & (line + r >= row0) & (line + r < row0 + n)
                        at_row = r % n
                        block = (rbuf[s, o, c, at_row:at_row + BORDER] if o
                                 else grad[at.block, s, c, at_row:at_row + BORDER])
                        term = jnp.where(inside, block.astype(F32), 0.0)
                        total = term if total is None else total + term
                    if away:
                        sbuf[s, c, r:r + BORDER, :] = total.astype(BF16)
                    else:
                        keep[s, c, r:r + BORDER, :] = total
            if away:
                ycopies[s] = remote(sbuf.at[s], ybuf.at[s], ysend.at[s], yrecv.at[s], at.partner)
                ycopies[s].start()
    first, last = at.tile == 0, at.tile == at.tiles - 1
    zcopies = {}
    for s in order:
        ycopies[s].wait_recv()
        for c in range(2):
            zout[s, 0, c] = (keep[s, c, :BORDER] + ybuf[s, c, :BORDER].astype(F32)).astype(BF16)
            zout[s, 1, c] = (keep[s, c, BORDER + rows:] + ybuf[s, c, BORDER + rows:].astype(F32)).astype(BF16)
        up = remote(zout.at[s, 0], zin.at[s, 0], zsend.at[s, 0], zrecv.at[s, 0], at.tile_peer(at.tiles - 1))
        down = remote(zout.at[s, 1], zin.at[s, 1], zsend.at[s, 1], zrecv.at[s, 1], at.tile_peer(1))
        zcopies[s] = (up, down)

        @pl.when(jnp.logical_not(first))
        def _():
            up.start()

        @pl.when(jnp.logical_not(last))
        def _():
            down.start()

        for c in range(2):
            for r in range(BORDER, BORDER + rows, BORDER):
                out[s, c, r - BORDER:r, :] = keep[s, c, r:r + BORDER] + ybuf[s, c, r:r + BORDER].astype(F32)
    for s in order:
        up, down = zcopies[s]

        @pl.when(jnp.logical_not(last))
        def _():
            up.wait_recv()
            for c in range(2):
                out[s, c, rows - BORDER:, :] += zin[s, 0, c].astype(F32)

        @pl.when(jnp.logical_not(first))
        def _():
            down.wait_recv()
            for c in range(2):
                out[s, c, :BORDER, :] += zin[s, 1, c].astype(F32)
            up.wait_send()

        @pl.when(jnp.logical_not(last))
        def _():
            down.wait_send()
    total = loss[...]
    for copy, o in zip(lcopies, range(1, at.tiles)):
        copy.wait_recv()
        total = total + lbuf[o]
    losses[...] = total
    for copy in list(xcopies.values()) + list(ycopies.values()) + lcopies:
        copy.wait_send()


def spread(grad, posall, loss, rows):
    group, slices, _, n, width = grad.shape
    tiles = lax.axis_size("tile")
    vmem = pl.BlockSpec(memory_space=pltpu.VMEM)
    dma = pltpu.SemaphoreType.DMA
    high = rows + 2 * BORDER
    return pl.pallas_call(
        functools.partial(spread_kernel, group),
        out_shape=(jax.ShapeDtypeStruct((slices, 2, rows, width), F32), jax.ShapeDtypeStruct((8, 128), F32)),
        in_specs=[vmem] * 3, out_specs=(vmem, vmem),
        scratch_shapes=[
            pltpu.VMEM((slices, group, 2, n, width), BF16), pltpu.VMEM((slices, 2, high, width), F32),
            pltpu.VMEM((slices, 2, high, width), BF16), pltpu.VMEM((slices, 2, high, width), BF16),
            pltpu.VMEM((slices, 2, 2, BORDER, width), BF16), pltpu.VMEM((slices, 2, 2, BORDER, width), BF16),
            pltpu.VMEM((tiles, 8, 128), F32),
            dma((tiles,)), dma((tiles,)), dma((slices, 2)), dma((slices, 2)), dma((slices,)), dma((slices,)),
            dma((slices, group)), dma((slices, group))],
        compiler_params=pltpu.CompilerParams(collective_id=1, has_side_effects=True, vmem_limit_bytes=24 << 20),
        name="spread",
    )(grad, posall, loss)


def extended(value, axis, dim, width):
    size, length = lax.axis_size(axis), value.shape[dim]
    up = [(i, i + 1) for i in range(size - 1)]
    down = [(j, i) for i, j in up]
    before = lax.ppermute(lax.slice_in_dim(value, length - width, length, axis=dim), axis, up)
    after = lax.ppermute(lax.slice_in_dim(value, 0, width, axis=dim), axis, down)
    return jnp.concatenate([before, value, after], axis=dim)


def fold_of(band, row0, col0, n, blocks):
    col, line = jnp.arange(n) < col0, (jnp.arange(n) < row0)[:, None]
    flat = jnp.where(col, band[..., n:], band[..., :n])
    over = jnp.pad(flat[..., n:, :], ((0, 0), (0, 0), (0, 2 * n - flat.shape[2]), (0, 0)))
    flat = jnp.where(line, over, flat[..., :n, :])
    return jnp.moveaxis(flat.reshape(flat.shape[:3] + (blocks, n // blocks)), 3, 0)


def unfold(grad, row0, col0, rows, cols):
    slices, n = grad.shape[1], grad.shape[3]
    flat = jnp.moveaxis(grad, 0, 3).reshape(slices, 2, n, n)
    r, c = jnp.arange(rows), jnp.arange(cols)
    inside = ((r >= row0) & (r < row0 + n))[:, None] & ((c >= col0) & (c < col0 + n))
    dense = jnp.concatenate([flat, flat[:, :, :rows - n]], axis=2)
    return jnp.where(inside, jnp.concatenate([dense, dense[..., :cols - n]], axis=3), 0)


def body(transmission, illumination, intensities, scan_positions, tile_owner):
    tile_index = lax.axis_index("tile")
    tile_rows, width = transmission.shape[2:]
    slots = tile_owner.shape[0]
    n = illumination.shape[-1]
    owned = tile_owner == tile_index
    chosen = jnp.sum(jnp.where(owned, jnp.arange(slots), 0)).astype(jnp.int32)
    usable = jnp.any(owned)
    place = jnp.sum(jnp.where(owned[:, None], scan_positions, 0), axis=0)
    pos = jnp.stack([place[0], place[1], usable.astype(jnp.int32), chosen])
    if width == 128 and lax.axis_size("probe") * width == 2 * n:
        postile = jnp.broadcast_to(jnp.pad(place, (0, 6))[:, None], (8, 128))
        fold, posall = collect(transmission, postile, n)
        grad, loss = compute(pos, fold, illumination, intensities)
        gradient, losses = spread(grad, posall, loss, tile_rows)
        return gradient, losses[:slots, 0]
    cols = lax.axis_size("probe") * width
    band = lax.all_gather(extended(transmission, "tile", 2, BORDER), "probe", axis=3, tiled=True)
    fold = fold_of(band, place[0], place[1], n, n // 128)
    grad, loss = compute(pos, fold, illumination, intensities)
    summed = unfold(grad, place[0], place[1], tile_rows + 2 * BORDER, cols)
    wide = lax.psum_scatter(summed, "probe", scatter_dimension=3, tiled=True).astype(F32)
    size = lax.axis_size("tile")
    up = [(i, i + 1) for i in range(size - 1)]
    down = [(j, i) for i, j in up]
    from_above = lax.ppermute(wide[:, :, :BORDER].astype(BF16), "tile", down).astype(F32)
    from_below = lax.ppermute(wide[:, :, tile_rows + BORDER:].astype(BF16), "tile", up).astype(F32)
    interior = wide[:, :, BORDER:BORDER + tile_rows]
    interior = interior.at[:, :, tile_rows - BORDER:].add(from_above)
    interior = interior.at[:, :, :BORDER].add(from_below)
    return interior, lax.psum(loss[:slots, 0], "tile")


def solution(mesh):
    in_specs = (P(None, None, "tile", "probe"), P(), P("probe", None, None), P("probe", None), P("probe"))
    out_specs = (P(None, None, "tile", "probe"), P("probe"))
    return jax.shard_map(body, mesh=mesh, in_specs=in_specs, out_specs=out_specs, check_vma=False)
```

time: 215 us -> 103 us (0.48)
  the two profiles are of different devices: /device:TPU:0 before, /device:TPU:1 now
where the time goes in v1:
time: 103 us; the launch traced here: 102 us
  Pallas kernels  87.9 us (85%)
  local copies, waits for them, and re-layouts  9.69 us (9%)
  other arithmetic  3.41 us (3%)
  between operations  1.33 us (1%)
    pallas_call x1, Pallas kernels, collect(): pl.pallas_call(functools.partial(collect_kernel, group), out_shape=(jax.S...  39 us
    pallas_call x1, Pallas kernels, spread(): pl.pallas_call(functools.partial(spread_kernel, group), out_shape=(jax.Sh...  33.8 us
    pallas_call x1, Pallas kernels, compute(): pl.pallas_call(compute_kernel, out_shape=(jax.ShapeDtypeStruct(fold.shape...  15 us
    unnamed x15, local copies, waits for them, and re-layouts  8.99 us

profile of v1, /device:TPU:1, one launch (start us, length us, event | category | flops | bytes accessed | tf_op | source)
XLA Modules:
  0.0 102.3 jit_solution(11493891994794676876)
XLA Ops:
  0.6 1.3 %fusion = (pred[]{:T(512)}, pred[2]{0:T(512)(128)(4,1)S(1)}) fusion(s32[2]{0:T(128)} %param.13, s32[]{:T(128)S(6)} %axis_index.12), kind=kLoop, calls=%fused_computation.5 | loop fusion | flops 3 | bytes 15 | tf_op jit(solution)/shard_map/reduce_or | solution.py:458
  2.6 0.6 select_reduce_fusion.1
  3.2 0.8 select_reduce_fusion
  4.0 0.7 pad_add_fusion.pos
  4.7 0.1 broadcast_in_dim.26.pos
  4.8 0.0 copy-start.2
  4.8 1.0 %copy-done.2 = bf16[2,2,512,128]{3,2,1,0:T(8,128)(2,1)S(1)} copy-done((bf16[2,2,512,128]{3,2,1,0:T(8,128)(2,1)S(1)}, bf16[2,2,512,128]{3,2,1,0:T(8,128)(2,1)}, u32[]{:S(2)}) %copy-start.2) | copy-done | bytes 524312
  5.8 39.0 %collect.1 = (bf16[4,2,2,512,128]{4,3,2,1,0:T(8,128)(2,1)S(1)}, s32[4,8,128]{2,1,0:T(8,128)S(1)}) custom-call(bf16[2,2,512,128]{3,2,1,0:T(8,128)(2,1)S(1)} %copy-done.2, s32[8,128]{1,0:T(8,128)S(1)} %broadcast_in_dim.26.pos), custom_call_target="tpu_custom_call" | custom-call | tf_op jit(solution)/shard_map/collect/pallas_call | solution.py:295
  44.8 0.0 copy-start
  44.9 1.6 %copy-done = f32[2,512,512]{2,1,0:T(8,128)S(1)} copy-done((f32[2,512,512]{2,1,0:T(8,128)S(1)}, f32[2,512,512]{2,1,0:T(8,128)}, u32[]{:S(2)}) %copy-start) | copy-done | bytes 2097176
  46.4 0.0 copy-start.1
  46.4 1.2 %copy-done.1 = bf16[2,512,512]{2,1,0:T(8,128)(2,1)S(1)} copy-done((bf16[2,512,512]{2,1,0:T(8,128)(2,1)S(1)}, bf16[2,512,512]{2,1,0:T(8,128)(2,1)}, u32[]{:S(2)}) %copy-start.1) | copy-done | bytes 1048600
  47.7 0.0 copy-start.3
  47.7 1.0 %copy-done.3 = bf16[512,512]{1,0:T(8,128)(2,1)S(1)} copy-done((bf16[512,512]{1,0:T(8,128)(2,1)S(1)}, bf16[512,512]{1,0:T(8,128)(2,1)}, u32[]{:S(2)}) %copy-start.3) | copy-done | bytes 524312
  48.7 0.0 copy-start.4
  48.7 1.0 %copy-done.4 = bf16[512,512]{1,0:T(8,128)(2,1)S(1)} copy-done((bf16[512,512]{1,0:T(8,128)(2,1)S(1)}, bf16[512,512]{1,0:T(8,128)(2,1)}, u32[]{:S(2)}) %copy-start.4) | copy-done | bytes 524312
  49.8 0.0 copy-start.5
  49.8 1.0 %copy-done.5 = bf16[512,512]{1,0:T(8,128)(2,1)S(1)} copy-done((bf16[512,512]{1,0:T(8,128)(2,1)S(1)}, bf16[512,512]{1,0:T(8,128)(2,1)}, u32[]{:S(2)}) %copy-start.5) | copy-done | bytes 524312
  50.8 0.0 copy-start.6
  50.8 1.0 %copy-done.6 = bf16[512,512]{1,0:T(8,128)(2,1)S(1)} copy-done((bf16[512,512]{1,0:T(8,128)(2,1)S(1)}, bf16[512,512]{1,0:T(8,128)(2,1)}, u32[]{:S(2)}) %copy-start.6) | copy-done | bytes 524312
  51.8 15.0 %probe_pass.1 = (bf16[4,2,2,512,128]{4,3,2,1,0:T(8,128)(2,1)S(1)}, f32[8,128]{1,0:T(8,128)S(1)}) custom-call(s32[4]{0:T(128)S(1)} %pad_add_fusion.pos, bf16[4,2,2,512,128]{4,3,2,1,0:T(8,128)(2,1)S(1)} %get-tuple-element.8.fold, bf16[2,512,512]{2,1,0:T(8,128)(2,1)S(1)} %copy-done.1, f32[2,512,512]{2,1,0:T(8,128)S(1)} %copy-done, ...), custom_call_target="tpu_custom_call" | custom-call | tf_op jit(solution)/shard_map/probe_pass/pallas_call | solution.py:145
  66.9 33.8 %spread.1 = (f32[2,2,512,128]{3,2,1,0:T(8,128)S(1)}, f32[8,128]{1,0:T(8,128)S(1)}) custom-call(bf16[4,2,2,512,128]{4,3,2,1,0:T(8,128)(2,1)S(1)} %get-tuple-element.9.grad, s32[4,8,128]{2,1,0:T(8,128)S(1)} %get-tuple-element.10.posall, f32[8,128]{1,0:T(8,128)S(1)} %get-tuple-element.11.loss), custom_call_target="tpu_custom_call" | custom-call | tf_op jit(solution)/shard_map/spread/pallas_call | solution.py:409
  100.7 0.6 slice_reduce_fusion
  101.3 1.0 copy.12
  (1 shorter events, 0.0 us)
Async XLA Ops:
  4.8 1.0 %copy-start.2 = (bf16[2,2,512,128]{3,2,1,0:T(8,128)(2,1)S(1)}, bf16[2,2,512,128]{3,2,1,0:T(8,128)(2,1)}, u32[]{:S(2)}) copy-start(bf16[2,2,512,128]{3,2,1,0:T(8,128)(2,1)} %tr.1) | copy-start | bytes 1572868
  44.8 1.6 %copy-start = (f32[2,512,512]{2,1,0:T(8,128)S(1)}, f32[2,512,512]{2,1,0:T(8,128)}, u32[]{:S(2)}) copy-start(f32[2,512,512]{2,1,0:T(8,128)} %meas.1) | copy-start | bytes 6291460
  46.4 1.2 %copy-start.1 = (bf16[2,512,512]{2,1,0:T(8,128)(2,1)S(1)}, bf16[2,512,512]{2,1,0:T(8,128)(2,1)}, u32[]{:S(2)}) copy-start(bf16[2,512,512]{2,1,0:T(8,128)(2,1)} %illum.1) | copy-start | bytes 3145732
  47.7 1.0 %copy-start.3 = (bf16[512,512]{1,0:T(8,128)(2,1)S(1)}, bf16[512,512]{1,0:T(8,128)(2,1)}, u32[]{:S(2)}) copy-start(bf16[512,512]{1,0:T(8,128)(2,1)} %constant.19.clone.qi) | copy-start | bytes 1572868
  48.7 1.0 %copy-start.4 = (bf16[512,512]{1,0:T(8,128)(2,1)S(1)}, bf16[512,512]{1,0:T(8,128)(2,1)}, u32[]{:S(2)}) copy-start(bf16[512,512]{1,0:T(8,128)(2,1)} %constant.18.clone.qr) | copy-start | bytes 1572868
  49.8 1.0 %copy-start.5 = (bf16[512,512]{1,0:T(8,128)(2,1)S(1)}, bf16[512,512]{1,0:T(8,128)(2,1)}, u32[]{:S(2)}) copy-start(bf16[512,512]{1,0:T(8,128)(2,1)} %constant.17.clone.wi) | copy-start | bytes 1572868
  50.8 1.0 %copy-start.6 = (bf16[512,512]{1,0:T(8,128)(2,1)S(1)}, bf16[512,512]{1,0:T(8,128)(2,1)}, u32[]{:S(2)}) copy-start(bf16[512,512]{1,0:T(8,128)(2,1)} %constant.16.clone.wr) | copy-start | bytes 1572868

commit v2 on v0

v2 whole, which is shorter than its diff:
```python
import functools
import math

import jax
import jax.numpy as jnp
import numpy as np
from jax import lax
from jax.experimental import pallas as pl
from jax.experimental.pallas import tpu as pltpu
from jax.sharding import PartitionSpec as P

BORDER = 128
FRESNEL = 0.25
F32 = jnp.float32
BF16 = jnp.bfloat16


def tables_of(n):
    k = np.arange(n)
    angle = -2.0 * np.pi * ((k[:, None] * k[None, :]) % n) / n
    wave = np.exp(1j * angle) / math.sqrt(n)
    freq = np.where(k < n // 2, k, k - n).astype(np.float64)
    h = np.exp(-1j * np.pi * FRESNEL * freq * freq / n)
    q = np.fft.ifft(h)
    prop = q[(k[:, None] - k[None, :]) % n]
    return [jnp.asarray(np.asarray(t, np.float32).astype(jnp.bfloat16))
            for t in (wave.real, wave.imag, prop.real, prop.imag)]


def compute_kernel(pos, fold, illum, meas, wr, wi, qr, qi, out, loss,
                   wide, x0, x1, obj, er, ei, ir, ii, msc, msem):
    n = illum.shape[-1]
    blocks, slices, width = fold.shape[0], fold.shape[1], fold.shape[-1]
    assert slices == 2
    step = n // 2
    row0, col0, usable, chosen = pos[0], pos[1], pos[2], pos[3]

    @pl.when(usable == 0)
    def _():
        loss[...] = jnp.zeros_like(loss)
        out[...] = jnp.zeros_like(out)

    def chunks(fn):
        def body(i, carry):
            fn(pl.multiple_of(i * step, step))
            return carry
        lax.fori_loop(0, n // step, body, 0)

    def transform(tr, ti, sign, emit):
        dot = functools.partial(jnp.dot, preferred_element_type=F32)

        def right(r):
            a, b = er[pl.ds(r, step), :], ei[pl.ds(r, step), :]
            rr, mm = dot(a, tr[...]), dot(b, ti[...])
            ir[pl.ds(r, step), :] = (rr - mm if sign > 0 else rr + mm).astype(BF16)
            rm, mr = dot(a, ti[...]), dot(b, tr[...])
            ii[pl.ds(r, step), :] = (mr + rm if sign > 0 else mr - rm).astype(BF16)

        chunks(right)

        def left(r):
            a, b = tr[pl.ds(r, step), :], ti[pl.ds(r, step), :]
            rr, mm = dot(a, ir[...]), dot(b, ii[...])
            rm, mr = dot(a, ii[...]), dot(b, ir[...])
            emit(r, rr - mm if sign > 0 else rr + mm, rm + mr if sign > 0 else rm - mr)

        chunks(left)

    @pl.when(usable != 0)
    def _():
        fetch = pltpu.make_async_copy(meas.at[chosen], msc, msem)
        fetch.start()
        wide[2 * n:, :] = jnp.zeros((8, n), F32)
        base = (n - row0) // 8 * 8
        turn = (72 - (n - row0 - base)) % 72
        for c in range(2):
            for r in range(0, n, 64):
                turned = pltpu.roll(illum[c, r:r + 64, :].astype(F32), col0 & (n - 1), 1)
                wide[r:r + 64, :] = turned
                wide[n + r:n + r + 64, :] = turned
            for r in range(0, n, 64):
                lines = wide[pl.ds(pl.multiple_of(base + r, 8), 72), :]
                x0[c, r:r + 64, :] = pltpu.roll(lines, turn, 0)[:64]

        for j in range(blocks):
            cols = slice(j * width, (j + 1) * width)
            for r in range(0, n, 128):
                rows = slice(r, r + 128)
                a, b = fold[j, 0, 0, rows].astype(F32), fold[j, 0, 1, rows].astype(F32)
                u, v = x0[0, rows, cols], x0[1, rows, cols]
                er[rows, cols] = (u * a - v * b).astype(BF16)
                ei[rows, cols] = (u * b + v * a).astype(BF16)
            obj[:, :, cols] = fold[j, 1]

        def emit_first(r, re, im):
            rows = pl.ds(r, step)
            x1[0, rows, :] = re
            x1[1, rows, :] = im
            a, b = obj[0, rows, :].astype(F32), obj[1, rows, :].astype(F32)
            er[rows, :] = (re * a - im * b).astype(BF16)
            ei[rows, :] = (re * b + im * a).astype(BF16)

        transform(qr, qi, 1, emit_first)
        fetch.wait()
        loss[...] = jnp.zeros_like(loss)

        def emit_far(r, re, im):
            rows = pl.ds(r, step)
            misfit = re * re + im * im - msc[rows, :]
            sq = jnp.sum((misfit * misfit).reshape(step // 8, 8, n), axis=0)
            loss[...] += functools.reduce(jnp.add, [sq[:, j:j + 128] for j in range(0, n, 128)])
            er[rows, :] = (misfit * re).astype(BF16)
            ei[rows, :] = (misfit * im).astype(BF16)

        transform(wr, wi, 1, emit_far)
        slot = lax.broadcasted_iota(jnp.int32, loss.shape, 0)
        loss[...] = jnp.where(slot == chosen, jnp.sum(loss[...]) / (n * n), 0.0)

        def place(s, r, parts):
            for c, g in enumerate(parts):
                for j in range(blocks):
                    out[j, s, c, pl.ds(r, step), :] = g[:, j * width:(j + 1) * width].astype(BF16)

        def emit_back(r, re, im):
            rows = pl.ds(r, step)
            u, v = x1[0, rows, :], x1[1, rows, :]
            place(1, r, (u * re + v * im, u * im - v * re))
            a, b = obj[0, rows, :].astype(F32), obj[1, rows, :].astype(F32)
            er[rows, :] = (a * re + b * im).astype(BF16)
            ei[rows, :] = (a * im - b * re).astype(BF16)

        transform(wr, wi, -1, emit_back)

        def emit_last(r, re, im):
            rows = pl.ds(r, step)
            u, v = x0[0, rows, :], x0[1, rows, :]
            place(0, r, (u * re + v * im, u * im - v * re))

        transform(qr, qi, -1, emit_last)


def compute(pos, fold, illumination, intensities):
    n = illumination.shape[-1]
    vmem = pl.BlockSpec(memory_space=pltpu.VMEM)
    return pl.pallas_call(
        compute_kernel,
        out_shape=(jax.ShapeDtypeStruct(fold.shape, BF16), jax.ShapeDtypeStruct((8, 128), F32)),
        in_specs=[pl.BlockSpec(memory_space=pltpu.SMEM), vmem, vmem,
                  pl.BlockSpec(memory_space=pl.ANY)] + [vmem] * 4,
        out_specs=(vmem, vmem),
        scratch_shapes=[
            pltpu.VMEM((2 * n + 8, n), F32), pltpu.VMEM((2, n, n), F32), pltpu.VMEM((2, n, n), F32),
            pltpu.VMEM((2, n, n), BF16)] + [pltpu.VMEM((n, n), BF16)] * 4 + [
            pltpu.VMEM((n, n), F32), pltpu.SemaphoreType.DMA],
        compiler_params=pltpu.CompilerParams(vmem_limit_bytes=40 << 20),
        name="probe_pass",
    )(pos, fold, illumination, intensities, *tables_of(n))


MESH = pl.DeviceIdType.MESH


class Places:
    def __init__(self, group):
        self.group, self.tiles = group, lax.axis_size("tile")
        self.me, self.tile = lax.axis_index("probe"), lax.axis_index("tile")
        self.half, self.block = self.me // group, lax.rem(self.me, group)
        self.partner = (lax.rem(self.me + group, 2 * group), self.tile)

    def peer(self, off):
        return (self.half * self.group + lax.rem(self.block + off, self.group), self.tile)

    def tile_peer(self, off):
        return (self.me, lax.rem(self.tile + off, self.tiles))

    def meet(self):
        barrier = pltpu.get_barrier_semaphore()
        others = ([self.partner] + [self.peer(o) for o in range(1, self.group)]
                  + [self.tile_peer(o) for o in range(1, self.tiles)])
        for other in others:
            pl.semaphore_signal(barrier, inc=1, device_id=other, device_id_type=MESH)
        pl.semaphore_wait(barrier, len(others))


def remote(src, dst, send, recv, device):
    return pltpu.make_async_remote_copy(src_ref=src, dst_ref=dst, send_sem=send, recv_sem=recv,
                                        device_id=device, device_id_type=MESH)


def fused_kernel(group, slots, tr, illum_hbm, meas_hbm, places, owners, wr_hbm, wi_hbm, qr_hbm, qi_hbm, out, losses,
                 ext, cbuf, fold, grad, rbuf, keep, sbuf, ybuf, zout, zin, pbuf, posall, loss, lbuf,
                 illum, meas, tables, x0, x1, er, ei, ir, ii,
                 local, psend, precv, zs, zr, msend, mrecv, ys, yr, xs, xr,
                 lsend, lrecv, zsend, zrecv, ysend, yrecv, xsend, xrecv):
    slices, _, rows, width = out.shape
    n = fold.shape[-2]
    extra = 2 * BORDER
    high = rows + extra
    step = n // 2
    dot = functools.partial(jnp.dot, preferred_element_type=F32)
    at = Places(group)
    first, last = at.tile == 0, at.tile == at.tiles - 1
    top, low, mid = slice(0, BORDER), slice(BORDER + rows, high), slice(BORDER, BORDER + rows)

    loads = [(tr.at[s], ext.at[s, 0, :, mid]) for s in range(slices)]
    loads += [(illum_hbm, illum), (qr_hbm, tables.at[0]), (qi_hbm, tables.at[1]), (wr_hbm, tables.at[2]),
              (wi_hbm, tables.at[3]), (meas_hbm, meas)]
    loads = [pltpu.make_async_copy(src, dst, local.at[i]) for i, (src, dst) in enumerate(loads)]
    for copy in loads:
        copy.start()
    owned = [owners[j] == at.tile for j in range(slots)]
    row0 = col0 = usable = chosen = jnp.int32(0)
    for j in range(slots):
        row0 = jnp.where(owned[j], places[j, 0], row0)
        col0 = jnp.where(owned[j], places[j, 1], col0)
        usable = jnp.where(owned[j], 1, usable)
        chosen = jnp.where(owned[j], j, chosen)
    sub = lax.broadcasted_iota(jnp.int32, (8, 128), 0)
    pbuf[...] = jnp.where(sub == 0, row0, col0)
    posall[0] = pbuf[...]
    at.meet()

    down = remote(tr.at[:, :, rows - BORDER:], ext.at[:, 0, :, top], zs.at[0], zr.at[0], at.tile_peer(1))
    up = remote(tr.at[:, :, :BORDER], ext.at[:, 0, :, low], zs.at[1], zr.at[1], at.tile_peer(at.tiles - 1))

    @pl.when(jnp.logical_not(last))
    def _():
        down.start()

    @pl.when(jnp.logical_not(first))
    def _():
        up.start()

    early = remote(tr.at[0, 0], ext.at[0, 1, 0, mid], msend, mrecv, at.partner)
    early.start()
    pcopies = [remote(pbuf, posall.at[o], psend.at[o], precv.at[o], at.peer(o)) for o in range(1, group)]
    for copy in pcopies:
        copy.start()

    @pl.when(first)
    def _():
        ext[:, 0, :, top, :] = jnp.zeros((slices, 2, BORDER, width), BF16)

    @pl.when(last)
    def _():
        ext[:, 0, :, low, :] = jnp.zeros((slices, 2, BORDER, width), BF16)

    for s in range(slices):
        loads[s].wait()

    @pl.when(jnp.logical_not(first))
    def _():
        down.wait_recv()

    @pl.when(jnp.logical_not(last))
    def _():
        up.wait_recv()

    yins = {}
    for s in range(slices):
        for c in range(2):
            parts = (top, low) if (s, c) == (0, 0) else (slice(0, high),)
            yins[s, c] = [remote(ext.at[s, 0, c, p], ext.at[s, 1, c, p], ys.at[s, c, i], yr.at[s, c, i], at.partner)
                          for i, p in enumerate(parts)]
            for copy in yins[s, c]:
                copy.start()
    yins[0, 0].append(early)

    loads[slices].wait()
    i = lax.broadcasted_iota(jnp.int32, (n, n), 0)
    j = lax.broadcasted_iota(jnp.int32, (n, n), 1)
    for target, line, lands, by in ((er, i, j, col0), (ei, j, i, row0)):
        moved = line + by
        target[...] = jnp.where(jnp.where(moved >= n, moved - n, moved) == lands, 1.0, 0.0).astype(BF16)
    for c in range(2):
        ir[...] = dot(illum[c], er[...]).astype(BF16)
        x0[c] = dot(ei[...], ir[...])

    for copy in pcopies:
        copy.wait_recv()
    lane = lax.broadcasted_iota(jnp.int32, (extra, width), 1) + at.block * width
    line = lax.broadcasted_iota(jnp.int32, (extra, width), 0)
    xins = {}
    for s in range(slices):
        for c in range(2):
            for copy in yins[s, c]:
                copy.wait_recv()
            for o in list(range(1, group)) + [0]:
                who = posall[(group - o) % group]
                prow, pcol = who[0:1, :width], who[1:2, :width]
                mine = jnp.where(lane < pcol, 1, 0) == at.half
                for r in range(0, n, extra):
                    v = jnp.where(mine, ext[s, 0, c, r:r + extra].astype(F32), ext[s, 1, c, r:r + extra].astype(F32))
                    if r + n < high:
                        w = jnp.where(mine, ext[s, 0, c, n + r:n + r + extra].astype(F32),
                                      ext[s, 1, c, n + r:n + r + extra].astype(F32))
                        v = jnp.where(line + r < prow, w, v)
                    if o:
                        cbuf[s, c, o, r:r + extra, :] = v.astype(BF16)
                    else:
                        fold[s, c, at.block, r:r + extra, :] = v.astype(BF16)
                if o:
                    xins[s, c, o] = remote(cbuf.at[s, c, o], fold.at[s, c, at.block], xs.at[s, c, o], xr.at[s, c, o],
                                           at.peer(o))
                    xins[s, c, o].start()

    def chunks(fn):
        def step_of(k, carry):
            fn(pl.multiple_of(k * step, step))
            return carry
        lax.fori_loop(0, n // step, step_of, 0)

    def transform(tr_at, ti_at, sign, emit):
        t_re, t_im = tables.at[tr_at], tables.at[ti_at]

        def right(r):
            a, b = er[pl.ds(r, step), :], ei[pl.ds(r, step), :]
            rr, mm = dot(a, t_re[...]), dot(b, t_im[...])
            ir[pl.ds(r, step), :] = (rr - mm if sign > 0 else rr + mm).astype(BF16)
            rm, mr = dot(a, t_im[...]), dot(b, t_re[...])
            ii[pl.ds(r, step), :] = (mr + rm if sign > 0 else mr - rm).astype(BF16)

        chunks(right)

        def left(r):
            a, b = t_re[pl.ds(r, step), :], t_im[pl.ds(r, step), :]
            rr, mm = dot(a, ir[...]), dot(b, ii[...])
            rm, mr = dot(a, ii[...]), dot(b, ir[...])
            emit(r, rr - mm if sign > 0 else rr + mm, rm + mr if sign > 0 else rm - mr)

        chunks(left)

    def exit_wave(s, wave):
        for c in range(2):
            for o in range(1, group):
                xins[s, c, o].wait_recv()
        for b in range(group):
            cols = slice(b * width, (b + 1) * width)
            for r in range(0, n, 128):
                part = slice(r, r + 128)
                p, q = fold[s, 0, b, part].astype(F32), fold[s, 1, b, part].astype(F32)
                u, v = wave[0, part, cols], wave[1, part, cols]
                er[part, cols] = (u * p - v * q).astype(BF16)
                ei[part, cols] = (u * q + v * p).astype(BF16)

    for copy in loads[slices + 1:slices + 3]:
        copy.wait()
    exit_wave(0, x0)

    def emit_first(r, re, im):
        x1[0, pl.ds(r, step), :] = re
        x1[1, pl.ds(r, step), :] = im

    transform(0, 1, 1, emit_first)
    for copy in loads[slices + 3:]:
        copy.wait()
    exit_wave(1, x1)
    loss[...] = jnp.zeros_like(loss)

    def emit_far(r, re, im):
        part = pl.ds(r, step)
        measured = meas[0, part, :]
        for k in range(1, slots):
            measured = jnp.where(chosen == k, meas[k, part, :], measured)
        misfit = jnp.where(usable == 1, re * re + im * im - measured, 0.0)
        sq = jnp.sum((misfit * misfit).reshape(step // 8, 8, n), axis=0)
        loss[...] += functools.reduce(jnp.add, [sq[:, k:k + 128] for k in range(0, n, 128)])
        er[part, :] = (misfit * re).astype(BF16)
        ei[part, :] = (misfit * im).astype(BF16)

    transform(2, 3, 1, emit_far)
    loss[...] = jnp.where(sub == chosen, jnp.sum(loss[...]) / (n * n), 0.0)

    def place(s, r, wave, re, im):
        u, v = wave[0, pl.ds(r, step), :], wave[1, pl.ds(r, step), :]
        for c, g in enumerate((u * re + v * im, u * im - v * re)):
            for b in range(group):
                grad[s, c, b, pl.ds(r, step), :] = g[:, b * width:(b + 1) * width].astype(BF16)

    def emit_back(r, re, im):
        part = pl.ds(r, step)
        place(1, r, x1, re, im)
        for b in range(group):
            cols = slice(b * width, (b + 1) * width)
            p, q = fold[1, 0, b, part, :].astype(F32), fold[1, 1, b, part, :].astype(F32)
            er[part, cols] = (p * re[:, cols] + q * im[:, cols]).astype(BF16)
            ei[part, cols] = (p * im[:, cols] - q * re[:, cols]).astype(BF16)

    xouts = {}

    def send(s):
        for c in range(2):
            for o in range(1, group):
                peer = lax.rem(at.block + o, group)
                xouts[s, c, o] = remote(grad.at[s, c, peer], rbuf.at[s, c, o], xsend.at[s, c, o], xrecv.at[s, c, o],
                                        at.peer(o))
                xouts[s, c, o].start()

    transform(2, 3, -1, emit_back)
    send(1)
    lcopies = [remote(loss, lbuf.at[o], lsend.at[o], lrecv.at[o], at.tile_peer(o)) for o in range(1, at.tiles)]
    for copy in lcopies:
        copy.start()
    transform(0, 1, -1, lambda r, re, im: place(0, r, x0, re, im))
    send(0)

    lane = lax.broadcasted_iota(jnp.int32, (BORDER, width), 1) + at.block * width
    line = lax.broadcasted_iota(jnp.int32, (BORDER, width), 0)
    order = [(s, c) for s in range(slices - 1, -1, -1) for c in range(2)]
    youts, zouts = {}, {}

    def add_up(s, c, away):
        cols = lane + (1 - at.half if away else at.half) * n
        for r in range(0, high, BORDER):
            total = None
            for o in range(group):
                who = posall[o]
                prow, pcol = who[0:1, :width], who[1:2, :width]
                inside = (cols >= pcol) & (cols < pcol + n) & (line + r >= prow) & (line + r < prow + n)
                k = r % n
                block = rbuf[s, c, o, k:k + BORDER] if o else grad[s, c, at.block, k:k + BORDER]
                term = jnp.where(inside, block.astype(F32), 0.0)
                total = term if total is None else total + term
            if away:
                sbuf[s, c, r:r + BORDER, :] = total.astype(BF16)
            else:
                keep[s, c, r:r + BORDER, :] = total

    def settle(s, c):
        youts[s, c].wait_recv()
        zout[s, c, 0] = (keep[s, c, top] + ybuf[s, c, top].astype(F32)).astype(BF16)
        zout[s, c, 1] = (keep[s, c, low] + ybuf[s, c, low].astype(F32)).astype(BF16)
        above = remote(zout.at[s, c, 0], zin.at[s, c, 0], zsend.at[s, c, 0], zrecv.at[s, c, 0],
                       at.tile_peer(at.tiles - 1))
        below = remote(zout.at[s, c, 1], zin.at[s, c, 1], zsend.at[s, c, 1], zrecv.at[s, c, 1], at.tile_peer(1))
        zouts[s, c] = (above, below)

        @pl.when(jnp.logical_not(first))
        def _():
            above.start()

        @pl.when(jnp.logical_not(last))
        def _():
            below.start()

        for r in range(BORDER, BORDER + rows, BORDER):
            out[s, c, r - BORDER:r, :] = keep[s, c, r:r + BORDER] + ybuf[s, c, r:r + BORDER].astype(F32)

    for k, (s, c) in enumerate(order):
        for o in range(1, group):
            xouts[s, c, o].wait_recv()
        add_up(s, c, True)
        youts[s, c] = remote(sbuf.at[s, c], ybuf.at[s, c], ysend.at[s, c], yrecv.at[s, c], at.partner)
        youts[s, c].start()
        add_up(s, c, False)
        if k:
            settle(*order[k - 1])
    settle(*order[-1])
    for s, c in order:
        above, below = zouts[s, c]

        @pl.when(jnp.logical_not(last))
        def _():
            above.wait_recv()
            out[s, c, rows - BORDER:, :] += zin[s, c, 0].astype(F32)

        @pl.when(jnp.logical_not(first))
        def _():
            below.wait_recv()
            out[s, c, :BORDER, :] += zin[s, c, 1].astype(F32)
            above.wait_send()

        @pl.when(jnp.logical_not(last))
        def _():
            below.wait_send()

    total = loss[...]
    for o, copy in zip(range(1, at.tiles), lcopies):
        copy.wait_recv()
        total = total + lbuf[o]
    losses[...] = total

    @pl.when(jnp.logical_not(last))
    def _():
        down.wait_send()

    @pl.when(jnp.logical_not(first))
    def _():
        up.wait_send()

    for copy in pcopies + lcopies + [c for pair in yins.values() for c in pair]:
        copy.wait_send()
    for group_of in (xins, xouts, youts):
        for copy in group_of.values():
            copy.wait_send()


def fused(transmission, illumination, intensities, scan_positions, tile_owner):
    slices, _, rows, width = transmission.shape
    n, slots = illumination.shape[-1], tile_owner.shape[0]
    group, tiles = n // width, lax.axis_size("tile")
    high = rows + 2 * BORDER
    vmem, smem, hbm = (pl.BlockSpec(memory_space=m) for m in (pltpu.VMEM, pltpu.SMEM, pl.ANY))
    dma = pltpu.SemaphoreType.DMA
    pair = (slices, 2)

    def buf(*shape, dtype=BF16):
        return pltpu.VMEM(shape, dtype)

    return pl.pallas_call(
        functools.partial(fused_kernel, group, slots),
        out_shape=(jax.ShapeDtypeStruct((slices, 2, rows, width), F32), jax.ShapeDtypeStruct((8, 128), F32)),
        in_specs=[hbm, hbm, hbm, smem, smem] + [hbm] * 4, out_specs=(vmem, vmem),
        scratch_shapes=[
            buf(slices, 2, 2, high, width), buf(*pair, group, n, width), buf(*pair, group, n, width),
            buf(*pair, group, n, width), buf(*pair, group, n, width), buf(*pair, high, width, dtype=F32),
            buf(*pair, high, width), buf(*pair, high, width), buf(*pair, 2, BORDER, width),
            buf(*pair, 2, BORDER, width), buf(8, 128, dtype=jnp.int32), buf(group, 8, 128, dtype=jnp.int32),
            buf(8, 128, dtype=F32), buf(tiles, 8, 128, dtype=F32),
            buf(2, n, n), buf(slots, n, n, dtype=F32), buf(4, n, n), buf(2, n, n, dtype=F32), buf(2, n, n, dtype=F32),
            buf(n, n), buf(n, n), buf(n, n), buf(n, n),
            dma((slices + 6,)), dma((group,)), dma((group,)), dma((2,)), dma((2,)), dma, dma,
            dma(pair + (2,)), dma(pair + (2,)), dma(pair + (group,)), dma(pair + (group,)),
            dma((tiles,)), dma((tiles,)), dma(pair + (2,)), dma(pair + (2,)), dma(pair), dma(pair),
            dma(pair + (group,)), dma(pair + (group,))],
        compiler_params=pltpu.CompilerParams(collective_id=0, has_side_effects=True, vmem_limit_bytes=60 << 20),
        name="fused_step",
    )(transmission, illumination, intensities, scan_positions, tile_owner, *tables_of(n))


def extended(value, axis, dim, width):
    size, length = lax.axis_size(axis), value.shape[dim]
    up = [(i, i + 1) for i in range(size - 1)]
    down = [(j, i) for i, j in up]
    before = lax.ppermute(lax.slice_in_dim(value, length - width, length, axis=dim), axis, up)
    after = lax.ppermute(lax.slice_in_dim(value, 0, width, axis=dim), axis, down)
    return jnp.concatenate([before, value, after], axis=dim)


def fold_of(band, row0, col0, n, blocks):
    col, line = jnp.arange(n) < col0, (jnp.arange(n) < row0)[:, None]
    flat = jnp.where(col, band[..., n:], band[..., :n])
    over = jnp.pad(flat[..., n:, :], ((0, 0), (0, 0), (0, 2 * n - flat.shape[2]), (0, 0)))
    flat = jnp.where(line, over, flat[..., :n, :])
    return jnp.moveaxis(flat.reshape(flat.shape[:3] + (blocks, n // blocks)), 3, 0)


def unfold(grad, row0, col0, rows, cols):
    slices, n = grad.shape[1], grad.shape[3]
    flat = jnp.moveaxis(grad, 0, 3).reshape(slices, 2, n, n)
    r, c = jnp.arange(rows), jnp.arange(cols)
    inside = ((r >= row0) & (r < row0 + n))[:, None] & ((c >= col0) & (c < col0 + n))
    dense = jnp.concatenate([flat, flat[:, :, :rows - n]], axis=2)
    return jnp.where(inside, jnp.concatenate([dense, dense[..., :cols - n]], axis=3), 0)


def body(transmission, illumination, intensities, scan_positions, tile_owner):
    tile_index = lax.axis_index("tile")
    tile_rows, width = transmission.shape[2:]
    slots = tile_owner.shape[0]
    n = illumination.shape[-1]
    owned = tile_owner == tile_index
    chosen = jnp.sum(jnp.where(owned, jnp.arange(slots), 0)).astype(jnp.int32)
    usable = jnp.any(owned)
    place = jnp.sum(jnp.where(owned[:, None], scan_positions, 0), axis=0)
    pos = jnp.stack([place[0], place[1], usable.astype(jnp.int32), chosen])
    if width == 128 and lax.axis_size("probe") * width == 2 * n:
        gradient, losses = fused(transmission, illumination, intensities, scan_positions, tile_owner)
        return gradient, losses[:slots, 0]
    cols = lax.axis_size("probe") * width
    band = lax.all_gather(extended(transmission, "tile", 2, BORDER), "probe", axis=3, tiled=True)
    fold = fold_of(band, place[0], place[1], n, n // 128)
    grad, loss = compute(pos, fold, illumination, intensities)
    summed = unfold(grad, place[0], place[1], tile_rows + 2 * BORDER, cols)
    wide = lax.psum_scatter(summed, "probe", scatter_dimension=3, tiled=True).astype(F32)
    size = lax.axis_size("tile")
    up = [(i, i + 1) for i in range(size - 1)]
    down = [(j, i) for i, j in up]
    from_above = lax.ppermute(wide[:, :, :BORDER].astype(BF16), "tile", down).astype(F32)
    from_below = lax.ppermute(wide[:, :, tile_rows + BORDER:].astype(BF16), "tile", up).astype(F32)
    interior = wide[:, :, BORDER:BORDER + tile_rows]
    interior = interior.at[:, :, tile_rows - BORDER:].add(from_above)
    interior = interior.at[:, :, :BORDER].add(from_below)
    return interior, lax.psum(loss[:slots, 0], "tile")


def solution(mesh):
    in_specs = (P(None, None, "tile", "probe"), P(), P("probe", None, None), P("probe", None), P("probe"))
    out_specs = (P(None, None, "tile", "probe"), P("probe"))
    return jax.shard_map(body, mesh=mesh, in_specs=in_specs, out_specs=out_specs, check_vma=False)
```

time: 215 us -> 80.4 us (0.37)
  waiting for transfers between devices: 112 us -> 0 us
  Pallas kernels: 22.1 us -> 76 us
  local copies, waits for them, and re-layouts: 37.1 us -> 3.56 us
  between operations: 15.5 us -> 0.64 us
  blocking collectives: 13.4 us -> 0 us
  starting transfers between devices: 8.92 us -> 0 us
  other arithmetic: 5.3 us -> 0 us
    unnamed x3 -> x0, waiting for transfers between devices: 60 us -> none
    pallas_call x1, Pallas kernels: 22.1 us -> 76 us  [fused(): pl.pallas_call(functools.partial(fused_kernel, group, slots), out_shape=(...]
    all_gather x1 -> x0, waiting for transfers between devices: 43.7 us -> none  [body(): lax.all_gather(extended(transmission, 'tile', 2, BORDER), 'probe', axis=3...]
    unnamed x12 -> x1, local copies, waits for them, and re-layouts: 36 us -> 2.26 us
    psum x1 -> x0, blocking collectives: 13.4 us -> none  [body(): return (interior, lax.psum(local, 'tile'))]
    ppermute x4 -> x0, starting transfers between devices: 8.85 us -> none  [the longest x1 4.96 us: extended(): lax.ppermute(lax.slice_in_dim(value, length - width, length, axis=dim), a...]
    ppermute x4 -> x0, waiting for transfers between devices: 8.02 us -> none  [the longest x1 4.13 us: extended(): lax.ppermute(lax.slice_in_dim(value, 0, width, axis=dim), axis, down)]
  transfers between devices with their start and end apart: 6 -> 0, of which waited for: 5 -> 0; matrix products, arithmetic and copies ran while one was open for 2% -> 0% of each run, Pallas kernels for 0% -> 0%
where the time goes in v2:
time: 80.4 us; the launch traced here: 80.2 us
  Pallas kernels  76 us (95%)
  local copies, waits for them, and re-layouts  3.56 us (4%)
    pallas_call x1, Pallas kernels, fused(): pl.pallas_call(functools.partial(fused_kernel, group, slots), out_shape=(...  76 us
    unnamed x1, local copies, waits for them, and re-layouts  2.26 us

profile of v2, /device:TPU:0, one launch (start us, length us, event | category | flops | bytes accessed | tf_op | source)
XLA Modules:
  0.0 80.2 jit_solution(673306351433198838)
XLA Ops:
  0.6 76.0 %fused_step.1 = (f32[2,2,512,128]{3,2,1,0:T(8,128)}, f32[8,128]{1,0:T(8,128)}) custom-call(bf16[2,2,512,128]{3,2,1,0:T(8,128)(2,1)} %tr.1, bf16[2,512,512]{2,1,0:T(8,128)(2,1)} %illum_hbm.1, f32[2,512,512]{2,1,0:T(8,128)} %meas_hbm.1, s32[2,2]{1,0:T(2,128)} %places.1, s32[2]{0:T(128)} %owners.1, bf16[512,512]{1,0:T(8,128)(2,1)} %constant.8.clone.wr_hbm, ...), custom_call_target="tpu_custom_call" | custom-call | tf_op jit(solution)/shard_map/fused_step/pallas_call | solution.py:510
  76.7 1.3 %slice_reduce_fusion = f32[2]{0:T(128)} fusion(f32[8,128]{1,0:T(8,128)} %get-tuple-element.5), kind=kLoop, calls=%fused_computation | loop fusion | bytes 16 | tf_op jit(solution)/shard_map/slice | solution.py:569
  78.0 2.3 %copy.12 = f32[2,2,512,128]{3,2,1,0:T(8,128)} copy(f32[2,2,512,128]{3,2,1,0:T(8,128)} %get-tuple-element.8) | data formatting | bytes 2097152

commit v3 on v2

--- a/solution.py
+++ b/solution.py
@@ -389,12 +389,13 @@
     xouts = {}
 
     def send(s):
-        for c in range(2):
+        for c, h in ((0, 0), (0, 1), (1, 0), (1, 1)):
+            lines = slice(h * step, (h + 1) * step)
             for o in range(1, group):
                 peer = lax.rem(at.block + o, group)
-                xouts[s, c, o] = remote(grad.at[s, c, peer], rbuf.at[s, c, o], xsend.at[s, c, o], xrecv.at[s, c, o],
-                                        at.peer(o))
-                xouts[s, c, o].start()
+                xouts[s, c, h, o] = remote(grad.at[s, c, peer, lines], rbuf.at[s, c, o, lines], xsend.at[s, c, h, o],
+                                           xrecv.at[s, c, h, o], at.peer(o))
+                xouts[s, c, h, o].start()
 
     transform(2, 3, -1, emit_back)
     send(1)
@@ -406,12 +407,13 @@
 
     lane = lax.broadcasted_iota(jnp.int32, (BORDER, width), 1) + at.block * width
     line = lax.broadcasted_iota(jnp.int32, (BORDER, width), 0)
-    order = [(s, c) for s in range(slices - 1, -1, -1) for c in range(2)]
+    order = [(s, c, h) for s in range(slices - 1, -1, -1) for c in range(2) for h in range(2)]
+    spans = ((slice(0, step), slice(n, high)), (slice(step, n),))
     youts, zouts = {}, {}
 
-    def add_up(s, c, away):
+    def add_up(s, c, h, away):
         cols = lane + (1 - at.half if away else at.half) * n
-        for r in range(0, high, BORDER):
+        for r in [r for p in spans[h] for r in range(p.start, p.stop, BORDER)]:
             total = None
             for o in range(group):
                 who = posall[o]
@@ -426,37 +428,41 @@
             else:
                 keep[s, c, r:r + BORDER, :] = total
 
-    def settle(s, c):
-        youts[s, c].wait_recv()
-        zout[s, c, 0] = (keep[s, c, top] + ybuf[s, c, top].astype(F32)).astype(BF16)
-        zout[s, c, 1] = (keep[s, c, low] + ybuf[s, c, low].astype(F32)).astype(BF16)
-        above = remote(zout.at[s, c, 0], zin.at[s, c, 0], zsend.at[s, c, 0], zrecv.at[s, c, 0],
-                       at.tile_peer(at.tiles - 1))
-        below = remote(zout.at[s, c, 1], zin.at[s, c, 1], zsend.at[s, c, 1], zrecv.at[s, c, 1], at.tile_peer(1))
-        zouts[s, c] = (above, below)
-
-        @pl.when(jnp.logical_not(first))
-        def _():
-            above.start()
-
-        @pl.when(jnp.logical_not(last))
-        def _():
-            below.start()
-
-        for r in range(BORDER, BORDER + rows, BORDER):
+    def settle(s, c, h):
+        for copy in youts[s, c, h]:
+            copy.wait_recv()
+        if h == 0:
+            zout[s, c, 0] = (keep[s, c, top] + ybuf[s, c, top].astype(F32)).astype(BF16)
+            zout[s, c, 1] = (keep[s, c, low] + ybuf[s, c, low].astype(F32)).astype(BF16)
+            above = remote(zout.at[s, c, 0], zin.at[s, c, 0], zsend.at[s, c, 0], zrecv.at[s, c, 0],
+                           at.tile_peer(at.tiles - 1))
+            below = remote(zout.at[s, c, 1], zin.at[s, c, 1], zsend.at[s, c, 1], zrecv.at[s, c, 1], at.tile_peer(1))
+            zouts[s, c] = (above, below)
+
+            @pl.when(jnp.logical_not(first))
+            def _():
+                above.start()
+
+            @pl.when(jnp.logical_not(last))
+            def _():
+                below.start()
+
+        for r in [r for p in spans[h] for r in range(p.start, p.stop, BORDER) if BORDER <= r < BORDER + rows]:
             out[s, c, r - BORDER:r, :] = keep[s, c, r:r + BORDER] + ybuf[s, c, r:r + BORDER].astype(F32)
 
-    for k, (s, c) in enumerate(order):
+    for k, (s, c, h) in enumerate(order):
         for o in range(1, group):
-            xouts[s, c, o].wait_recv()
-        add_up(s, c, True)
-        youts[s, c] = remote(sbuf.at[s, c], ybuf.at[s, c], ysend.at[s, c], yrecv.at[s, c], at.partner)
-        youts[s, c].start()
-        add_up(s, c, False)
+            xouts[s, c, h, o].wait_recv()
+        add_up(s, c, h, True)
+        youts[s, c, h] = [remote(sbuf.at[s, c, p], ybuf.at[s, c, p], ysend.at[s, c, h + i * 2], yrecv.at[s, c, h + i * 2],
+                                 at.partner) for i, p in enumerate(spans[h])]
+        for copy in youts[s, c, h]:
+            copy.start()
+        add_up(s, c, h, False)
         if k:
             settle(*order[k - 1])
     settle(*order[-1])
-    for s, c in order:
+    for s, c in zouts:
         above, below = zouts[s, c]
 
         @pl.when(jnp.logical_not(last))
@@ -490,7 +496,9 @@
 
     for copy in pcopies + lcopies + [c for pair in yins.values() for c in pair]:
         copy.wait_send()
-    for group_of in (xins, xouts, youts):
+    for copy in [c for pair in youts.values() for c in pair]:
+        copy.wait_send()
+    for group_of in (xins, xouts):
         for copy in group_of.values():
             copy.wait_send()
 
@@ -521,8 +529,8 @@
             buf(n, n), buf(n, n), buf(n, n), buf(n, n),
             dma((slices + 6,)), dma((group,)), dma((group,)), dma((2,)), dma((2,)), dma, dma,
             dma(pair + (2,)), dma(pair + (2,)), dma(pair + (group,)), dma(pair + (group,)),
-            dma((tiles,)), dma((tiles,)), dma(pair + (2,)), dma(pair + (2,)), dma(pair), dma(pair),
-            dma(pair + (group,)), dma(pair + (group,))],
+            dma((tiles,)), dma((tiles,)), dma(pair + (2,)), dma(pair + (2,)), dma(pair + (3,)), dma(pair + (3,)),
+            dma(pair + (2, group)), dma(pair + (2, group))],
         compiler_params=pltpu.CompilerParams(collective_id=0, has_side_effects=True, vmem_limit_bytes=60 << 20),
         name="fused_step",
     )(transmission, illumination, intensities, scan_positions, tile_owner, *tables_of(n))

time: 80.4 us -> 78.6 us (0.978)
  Pallas kernels: 76 us -> 74.1 us
    pallas_call x1, Pallas kernels: 76 us -> 74.1 us  [fused(): pl.pallas_call(functools.partial(fused_kernel, group, slots), out_shape=(...]
where the time goes in v3:
time: 78.6 us; the launch traced here: 78.3 us
  Pallas kernels  74.1 us (94%)
  local copies, waits for them, and re-layouts  3.56 us (5%)
    pallas_call x1, Pallas kernels, fused(): pl.pallas_call(functools.partial(fused_kernel, group, slots), out_shape=(...  74.1 us
    unnamed x1, local copies, waits for them, and re-layouts  2.26 us

profile of v3, /device:TPU:0, one launch (start us, length us, event | category | flops | bytes accessed | tf_op | source)
XLA Modules:
  0.0 78.3 jit_solution(7745958751987608034)
XLA Ops:
  0.6 74.1 %fused_step.1 = (f32[2,2,512,128]{3,2,1,0:T(8,128)}, f32[8,128]{1,0:T(8,128)}) custom-call(bf16[2,2,512,128]{3,2,1,0:T(8,128)(2,1)} %tr.1, bf16[2,512,512]{2,1,0:T(8,128)(2,1)} %illum_hbm.1, f32[2,512,512]{2,1,0:T(8,128)} %meas_hbm.1, s32[2,2]{1,0:T(2,128)} %places.1, s32[2]{0:T(128)} %owners.1, bf16[512,512]{1,0:T(8,128)(2,1)} %constant.8.clone.wr_hbm, ...), custom_call_target="tpu_custom_call" | custom-call | tf_op jit(solution)/shard_map/fused_step/pallas_call | solution.py:518
  74.8 1.3 %slice_reduce_fusion = f32[2]{0:T(128)} fusion(f32[8,128]{1,0:T(8,128)} %get-tuple-element.5), kind=kLoop, calls=%fused_computation | loop fusion | bytes 16 | tf_op jit(solution)/shard_map/slice | solution.py:577
  76.1 2.3 %copy.12 = f32[2,2,512,128]{3,2,1,0:T(8,128)} copy(f32[2,2,512,128]{3,2,1,0:T(8,128)} %get-tuple-element.8) | data formatting | bytes 2097152
